TPU v7x, 32 devices: a whole 2x2x4 slice. The times are simulated.
32 devices in a mesh: seq: 16 (over z, y, core), mp: 2 (over x).
Axes of the slice: x: 2, y: 2, z: 4, core: 2. Of those that a mesh axis runs over, the one named last changes fastest.
Arguments:
- tokens: float32 [8192, 1024], P('seq'), may hold values from -6 to 6
- window_state: float32 [2, 1024, 16], P(None, ('seq', 'mp')), may hold values from -6 to 6
- norm1_gain: float32 [1024], replicated, may hold values from 0.5 to 1.5
- norm1_bias: float32 [1024], replicated, may hold values from -3 to 3
- in_coef: float32 [1024, 16], P(('seq', 'mp')), may hold values from -0.375 to 0.375
- out_coef: float32 [1024, 16], P(('seq', 'mp')), may hold values from -4 to 4
- decay_rate: float32 [1024, 16], P(('seq', 'mp')), may hold values from 6.1035156e-05 to 0.04
- skip_gain: float32 [1024], P(('seq', 'mp')), may hold values from 0.5 to 1.5
- qkv_weight: bfloat16 [3, 1024, 1024], P(None, None, 'mp'), may hold values from -0.1875 to 0.1875
- out_weight: bfloat16 [1024, 1024], P('mp'), may hold values from -0.75 to 0.75
- norm2_gain: float32 [1024], replicated, may hold values from 0.5 to 1.5
- norm2_bias: float32 [1024], replicated, may hold values from -3 to 3
- up_weight: bfloat16 [1024, 4096], P(None, 'mp'), may hold values from -0.1875 to 0.1875
- up_bias: float32 [4096], P('mp'), may hold values from -3 to 3
- down_weight: bfloat16 [4096, 1024], P('mp'), may hold values from -0.1875 to 0.1875
- down_bias: float32 [1024], replicated, may hold values from -3 to 3
- cotangent: float32 [8192, 1024], P('seq'), may hold values from -6 to 6
Outputs:
- result: float32 [8192, 1024], P('seq')
- grad_tokens: float32 [8192, 1024], P('seq')
- grad_norm1_gain: float32 [1024], replicated
- grad_norm1_bias: float32 [1024], replicated
- grad_in_coef: float32 [1024, 16], P(('seq', 'mp'))
- grad_out_coef: float32 [1024, 16], P(('seq', 'mp'))
- grad_decay_rate: float32 [1024, 16], P(('seq', 'mp'))
- grad_skip_gain: float32 [1024], P(('seq', 'mp'))
- grad_qkv_weight: float32 [3, 1024, 1024], P(None, None, 'mp')
- grad_out_weight: float32 [1024, 1024], P('mp')
- grad_norm2_gain: float32 [1024], replicated
- grad_norm2_bias: float32 [1024], replicated
- grad_up_weight: float32 [1024, 4096], P(None, 'mp')
- grad_up_bias: float32 [4096], P('mp')
- grad_down_weight: float32 [4096, 1024], P('mp')
- grad_down_bias: float32 [1024], replicated
All inputs are finite; a program needn't handle non-finite values.
Results may differ from a plain program's by a relative error of at most 0.002.
Values sent between devices are 32-bit elements; how exact they have to be, the bound alone decides.
No kernel may reach another device: no remote copies, remote signals or barrier semaphores. Data moves between devices by JAX's collectives and lax.ppermute only.
A program may use at most 192 MiB of HBM per device.

v0:
```python
import math
import jax
import jax.numpy as jnp
from jax import lax
from jax.sharding import PartitionSpec as P

HDIM = 128
BLOCK = 512
CTX = 128
LEN = 4096
epsilon = 1e-05


def from_behind(block, axis, distance):
    devices = range(lax.axis_size(axis))
    route = [(i - distance, i) for i in devices if i - distance in devices]
    return lax.ppermute(block, axis, route)


def product(form, left, right):
    return jnp.einsum(form, left, right, precision=lax.Precision.HIGHEST)


def layer_norm(value, gain, bias):
    center = value - jnp.mean(value, axis=-1, keepdims=True)
    spread = jnp.mean(center * center, axis=-1, keepdims=True)
    return center * lax.rsqrt(spread + epsilon) * gain + bias


def angle_table(count_rows, count_cols, modulus):
    left = jnp.arange(count_rows, dtype=jnp.int32)[:, None]
    right = jnp.arange(count_cols, dtype=jnp.int32)[None, :]
    phase = left * right % modulus
    angle = phase.astype(jnp.float32) * (2.0 * math.pi / modulus)
    return (jnp.cos(angle), jnp.sin(angle))


def forward_dft(signal, tables):
    cos_one, sin_one, cos_twid, sin_twid, cos_two, sin_two = tables
    first_re = product("...ab,ak->...kb", signal, cos_one)
    first_im = -product("...ab,ak->...kb", signal, sin_one)
    twid_re = first_re * cos_twid + first_im * sin_twid
    twid_im = first_im * cos_twid - first_re * sin_twid
    spec_re = product("...kb,bm->...km", twid_re, cos_two) + product(
        "...kb,bm->...km", twid_im, sin_two
    )
    spec_im = product("...kb,bm->...km", twid_im, cos_two) - product(
        "...kb,bm->...km", twid_re, sin_two
    )
    return (spec_re, spec_im)


def inverse_dft(spec_re, spec_im, tables, total):
    cos_one, sin_one, cos_twid, sin_twid, cos_two, sin_two = tables
    back_re = product("...km,mb->...kb", spec_re, cos_two) - product(
        "...km,mb->...kb", spec_im, sin_two
    )
    back_im = product("...km,mb->...kb", spec_re, sin_two) + product(
        "...km,mb->...kb", spec_im, cos_two
    )
    turn_re = back_re * cos_twid - back_im * sin_twid
    turn_im = back_re * sin_twid + back_im * cos_twid
    real_part = product("...kb,ka->...ab", turn_re, cos_one) - product(
        "...kb,ka->...ab", turn_im, sin_one
    )
    return real_part / total


def causal_conv(signal, kernel):
    channels, windows, length = signal.shape
    total = 2 * length
    bits = total.bit_length() - 1
    cols_count = 1 << bits - bits // 2
    rows_count = total // cols_count
    cos_one, sin_one = angle_table(rows_count, rows_count, rows_count)
    cos_twid, sin_twid = angle_table(rows_count, cols_count, total)
    cos_two, sin_two = angle_table(cols_count, cols_count, cols_count)
    tables = (cos_one, sin_one, cos_twid, sin_twid, cos_two, sin_two)
    padded = jnp.concatenate([signal, jnp.zeros_like(signal)], -1).reshape(
        channels, windows, rows_count, cols_count
    )
    kern_pad = jnp.concatenate([kernel, jnp.zeros_like(kernel)], -1).reshape(
        channels, 1, rows_count, cols_count
    )
    sig_re, sig_im = forward_dft(padded, tables)
    ker_re, ker_im = forward_dft(kern_pad, tables)
    prod_re = sig_re * ker_re - sig_im * ker_im
    prod_im = sig_re * ker_im + sig_im * ker_re
    whole = inverse_dft(prod_re, prod_im, tables, total).reshape(channels, windows, total)
    return whole[:, :, :length]


def ssm_local(time_rows, in_coef, out_coef, decay_rate, skip_gain, window_state):
    channels = time_rows.shape[0]
    windows = time_rows.shape[1] // LEN
    signal = time_rows.reshape(channels, windows, LEN)
    steps_t = jnp.arange(LEN).astype(jnp.float32)
    fading = jnp.exp(-decay_rate[:, :, None] * steps_t)
    kernel = product("cn,cnt->ct", in_coef * out_coef, fading)
    shifted = fading * jnp.exp(-decay_rate)[:, :, None]
    start = jnp.einsum(
        "cn,scn,cnt->cst", out_coef, window_state, shifted, precision=lax.Precision.HIGHEST
    )
    conv = causal_conv(signal, kernel)
    return (conv + skip_gain[:, None, None] * signal + start).reshape(channels, windows * LEN)


def attend_local(normed, context, qkv, out_w, ctx_ok):
    rows_here, model_width = normed.shape
    inner = qkv.shape[2]
    blocks = rows_here // BLOCK
    heads_here = inner // HDIM
    highest = lax.Precision.HIGHEST
    query = jnp.dot(normed, qkv[0], precision=highest).reshape(blocks, BLOCK, heads_here, HDIM)
    key_self = jnp.dot(normed, qkv[1], precision=highest).reshape(blocks, BLOCK, heads_here, HDIM)
    value_self = jnp.dot(normed, qkv[2], precision=highest).reshape(blocks, BLOCK, heads_here, HDIM)
    key_ctx = product("dbc,de->bce", context, qkv[1]).reshape(blocks, CTX, heads_here, HDIM)
    value_ctx = product("dbc,de->bce", context, qkv[2]).reshape(blocks, CTX, heads_here, HDIM)
    keys = jnp.concatenate([key_ctx, key_self], 1)
    values = jnp.concatenate([value_ctx, value_self], 1)
    scores = product("bqhe,bkhe->bhqk", query, keys) * HDIM ** (-0.5)
    rows_q = jnp.arange(BLOCK)[:, None]
    cols_k = jnp.arange(CTX + BLOCK)[None, :]
    allowed = jnp.where(
        cols_k < CTX, ctx_ok[:, None, None, None], (cols_k - CTX <= rows_q)[None, None]
    )
    scores = jnp.where(allowed, scores, -1e30)
    probs = jax.nn.softmax(scores, axis=-1)
    heads = product("bhqk,bkhe->bqhe", probs, values).reshape(rows_here, inner)
    return jnp.dot(heads, out_w, precision=highest)


def feed_local(normed2, up_w, up_b, down_w):
    highest = lax.Precision.HIGHEST
    hidden = jax.nn.gelu(jnp.dot(normed2, up_w, precision=highest) + up_b, approximate=False)
    return jnp.dot(hidden, down_w, precision=highest)


def sum_feed_grads(grad_up, grad_up_bias, grad_down, grad_down_bias):
    return lax.psum((grad_up, grad_up_bias, grad_down, grad_down_bias), "seq")


def per_device(
    tokens,
    window_state,
    norm1_gain,
    norm1_bias,
    in_coef,
    out_coef,
    decay_rate,
    skip_gain,
    qkv_weight,
    out_weight,
    norm2_gain,
    norm2_bias,
    up_weight,
    up_bias,
    down_weight,
    down_bias,
    cotangent,
):
    count_seq = lax.axis_size("seq")
    count_mp = lax.axis_size("mp")
    place_seq = lax.axis_index("seq")
    place_mp = lax.axis_index("mp")
    rows_here, model_width = tokens.shape
    blocks_here = rows_here // BLOCK
    channels = in_coef.shape[0]
    qkv_full = qkv_weight.astype(jnp.float32)
    out_full = out_weight.astype(jnp.float32)
    up_full = up_weight.astype(jnp.float32)
    down_full = down_weight.astype(jnp.float32)
    normed, norm1_pull = jax.vjp(layer_norm, tokens, norm1_gain, norm1_bias)
    grouped = normed.reshape(rows_here, count_seq, count_mp, channels)
    own_half = lax.dynamic_index_in_dim(grouped, place_mp, axis=2, keepdims=False)
    outgoing = jnp.transpose(own_half, (1, 2, 0)).reshape(count_seq * channels, rows_here)
    time_in = lax.all_to_all(outgoing, "seq", split_axis=0, concat_axis=1, tiled=True)

    def ssm_piece(time_rows, coef_in, coef_out, rates, skips):
        return ssm_local(time_rows, coef_in, coef_out, rates, skips, window_state)

    time_out, ssm_pull = jax.vjp(ssm_piece, time_in, in_coef, out_coef, decay_rate, skip_gain)
    returned = lax.all_to_all(time_out, "seq", split_axis=1, concat_axis=0, tiled=True)
    width_back = returned.shape[1]
    halves = lax.all_gather(
        returned.reshape(count_seq, 1, channels, width_back), "mp", axis=1, tiled=True
    )
    joined = halves.reshape(model_width, width_back)
    tail = from_behind(joined[:, rows_here - CTX :], "seq", 1)
    extended = jnp.concatenate([tail, joined], 1)
    context = extended[:, :rows_here].reshape(model_width, blocks_here, BLOCK)[:, :, :CTX]
    block_start = (place_seq * rows_here + jnp.arange(blocks_here) * BLOCK) % LEN
    ctx_ok = block_start > 0

    def attend_piece(normed_in, context_in, qkv_in, out_in):
        return attend_local(normed_in, context_in, qkv_in, out_in, ctx_ok)

    attn_part = attend_piece(normed, context, qkv_full, out_full)
    mixed = tokens + lax.psum(attn_part, "mp")
    normed2, norm2_pull = jax.vjp(layer_norm, mixed, norm2_gain, norm2_bias)
    feed_part = feed_local(normed2, up_full, up_bias, down_full)
    result = mixed + lax.psum(feed_part, "mp") + down_bias
    grad_down_bias = jnp.sum(cotangent, axis=0)
    unused_feed, feed_pull = jax.vjp(feed_local, normed2, up_full, up_bias, down_full)
    grad_normed2_part, grad_up, grad_up_bias, grad_down = feed_pull(cotangent)
    grad_normed2 = lax.psum(grad_normed2_part, "mp")
    grad_mixed_norm, grad_gain2, grad_bias2 = norm2_pull(grad_normed2)
    grad_mixed = cotangent + grad_mixed_norm
    unused_attn, attend_pull = jax.vjp(attend_piece, normed, context, qkv_full, out_full)
    grad_normed_part, grad_context, grad_qkv, grad_out = attend_pull(grad_mixed)
    spread_rows = jnp.pad(grad_context, ((0, 0), (0, 0), (0, BLOCK - CTX))).reshape(
        model_width, rows_here
    )
    grad_extended = jnp.concatenate([spread_rows, jnp.zeros((model_width, CTX), jnp.float32)], 1)
    grad_tail = from_behind(grad_extended[:, :CTX], "seq", -1)
    grad_joined = grad_extended[:, CTX:] + jnp.pad(grad_tail, ((0, 0), (rows_here - CTX, 0)))
    width_grad = grad_joined.shape[1]
    grad_half = lax.psum_scatter(
        grad_joined.reshape(count_seq, count_mp, channels, width_grad),
        "mp",
        scatter_dimension=1,
        tiled=True,
    )
    grad_time = lax.all_to_all(
        grad_half.reshape(count_seq * channels, width_grad),
        "seq",
        split_axis=0,
        concat_axis=1,
        tiled=True,
    )
    grad_time_in, grad_in_coef, grad_out_coef, grad_decay, grad_skip = ssm_pull(grad_time)
    grad_back = lax.all_to_all(grad_time_in, "seq", split_axis=1, concat_axis=0, tiled=True)
    selector = (jnp.arange(count_mp) == place_mp).astype(jnp.float32)
    placed = grad_back.reshape(count_seq, 1, channels, rows_here) * selector[None, :, None, None]
    placed_rows = jnp.transpose(placed.reshape(model_width, rows_here))
    grad_normed = lax.psum(grad_normed_part + placed_rows, "mp")
    grad_tokens_norm, grad_gain1, grad_bias1 = norm1_pull(grad_normed)
    grad_tokens = grad_mixed + grad_tokens_norm
    feed_sums = sum_feed_grads(grad_up, grad_up_bias, grad_down, grad_down_bias)
    rest_sums = lax.psum(
        (grad_gain1, grad_bias1, grad_qkv, grad_out, grad_gain2, grad_bias2), "seq"
    )
    return (
        result,
        grad_tokens,
        rest_sums[0],
        rest_sums[1],
        grad_in_coef,
        grad_out_coef,
        grad_decay,
        grad_skip,
        rest_sums[2],
        rest_sums[3],
        rest_sums[4],
        rest_sums[5],
        feed_sums[0],
        feed_sums[1],
        feed_sums[2],
        feed_sums[3],
    )


def solution(mesh):
    placed = (
        P("seq", None),
        P(None, ("seq", "mp"), None),
        P(),
        P(),
        P(("seq", "mp"), None),
        P(("seq", "mp"), None),
        P(("seq", "mp"), None),
        P(("seq", "mp")),
        P(None, None, "mp"),
        P("mp", None),
        P(),
        P(),
        P(None, "mp"),
        P("mp"),
        P("mp", None),
        P(),
        P("seq", None),
    )
    return jax.shard_map(
        per_device,
        mesh=mesh,
        in_specs=placed,
        out_specs=(
            P("seq", None),
            P("seq", None),
            P(),
            P(),
            P(("seq", "mp"), None),
            P(("seq", "mp"), None),
            P(("seq", "mp"), None),
            P(("seq", "mp")),
            P(None, None, "mp"),
            P("mp", None),
            P(),
            P(),
            P(None, "mp"),
            P("mp"),
            P("mp", None),
            P(),
        ),
        check_vma=False,
    )
```

profile of v0, /device:TPU:0, one launch (start us, length us, event | category | flops | bytes accessed | tf_op | source)
XLA Modules:
  0.0 1192.9 jit_solution(4121227456708853096)
XLA Ops:
  15.8 7.4 all-to-all-start
  23.6 5.3 fusion.2
  39.0 7.2 all-to-all-done
  93.2 7.8 fusion.8
  105.9 31.6 %all_to_all.61 = f32[32,16,512]{2,0,1:T(8,128)} all-to-all(f32[32,16,512]{2,0,1:T(8,128)S(1)} %copy.94), channel_id=1, replica_groups=mesh['seq'=16,'mp'=2] {'seq'}, dimensions={1} | all-to-all | bytes 2097152 | tf_op jit(solution)/shard_map/all_to_all | solution.py:183
  155.1 16.1 %all-gather.3.cloned.1.call-done = f32[16,64,512]{2,1,0:T(8,128)} async-done(((f32[16,32,512]{2,1,0:T(8,128)}), f32[16,64,512]{2,1,0:T(8,128)}) %all-gather.3.cloned.1.call-update) | async-done | bytes 2097168 | tf_op jit(solution)/shard_map/all_gather | solution.py:185
  184.1 5.5 fusion.7
  192.0 6.4 fusion.28
  202.8 67.9 %all-reduce.21.cloned.1.call-done = f32[512,1024]{1,0:T(8,128)} async-done(((f32[512,1024]{1,0:T(8,128)}), f32[512,1024]{1,0:T(8,128)}) %all-reduce.21.cloned.1.call-update) | async-done | bytes 2097168 | tf_op jit(solution)/shard_map/psum | solution.py:199
  274.6 7.2 fusion.78
  281.9 19.5 %fusion.441 = (f32[2048]{0:T(1024)}, f32[512,2048]{1,0:T(8,128)S(1)}, f32[512,2048]{1,0:T(8,128)}) fusion(f32[512,2048]{1,0:T(8,128)S(1)} %fusion.78, f32[2048]{0:T(1024)S(1)} %copy-done.116, f32[512,1024]{1,0:T(8,128)S(1)} %copy-done.48, bf16[2048,1024]{1,0:T(8,128)(2,1)S(1)} %copy-done.125), kind=kOutput, calls=%fused_computation.500 | convolution fusion | flops 12961445888 | bytes 18890752 | tf_op jit(solution)/shard_map/transpose(jvp())/dot_general | solution.py:136
  303.4 8.0 fusion.450
  312.5 62.0 %all-reduce.23.cloned.1.call-done = f32[512,1024]{1,0:T(8,128)} async-done(((f32[512,1024]{1,0:T(8,128)}), f32[512,1024]{1,0:T(8,128)}) %all-reduce.23.cloned.1.call-update) | async-done | bytes 2097168 | tf_op jit(solution)/shard_map/psum | solution.py:206
  392.5 8.2 multiply_reduce_fusion.2
  416.8 68.0 %all-reduce.25.cloned.1.call-done = f32[16,2,32,512]{3,2,1,0:T(8,128)} async-done(((f32[16,2,32,512]{3,2,1,0:T(8,128)}), f32[16,2,32,512]{3,2,1,0:T(8,128)}) %all-reduce.25.cloned.1.call-update) | async-done | bytes 2097168
  486.8 30.3 %all_to_all.62 = f32[16,32,512]{2,1,0:T(8,128)S(1)} all-to-all(f32[16,32,512]{2,1,0:T(8,128)S(1)} %dynamic-slice_bitcast_fusion), channel_id=1, replica_groups=mesh['seq'=16,'mp'=2] {'seq'}, dimensions={0} | all-to-all | bytes 2097152 | tf_op jit(solution)/shard_map/all_to_all | solution.py:224
  536.6 5.0 multiply_reduce_fusion.4
  562.6 5.0 all-to-all-start.3
  567.8 12.2 %fusion.106 = f32[512,1024]{1,0:T(8,128)} fusion(bf16[2048,1024]{1,0:T(8,128)(2,1)} %param.31, f32[512,2048]{1,0:T(8,128)} %get-tuple-element.58, f32[512,2048]{1,0:T(8,128)} %copy-done.63, f32[2048]{0:T(1024)S(1)} %copy-done.117), kind=kOutput, calls=%fused_computation.157 | convolution fusion | flops 12888047616 | bytes 14688256 | tf_op jit(solution)/shard_map/dot_general | solution.py:136
  592.0 5.6 fusion.109
  602.3 8.1 bitcast_add_fusion
  612.0 17.8 %fusion.77 = f32[1024,2048]{1,0:T(8,128)} fusion(f32[512,2048]{1,0:T(8,128)} %copy-done.129, f32[512,1024]{1,0:T(8,128)S(1)} %copy-done.19, f32[1024]{0:T(1024)S(1)} %copy-done.127, f32[1024]{0:T(1024)S(1)} %copy-done.115, f32[512]{0:T(512)S(1)} %copy-done.99, f32[512]{0:T(512)S(1)} %copy-done.96), kind=kOutput, calls=%fused_computation.127 | convolution fusion | flops 12886999040 | bytes 14692352 | tf_op jit(solution)/shard_map/transpose(jvp())/dot_general | solution.py:135
  629.9 16.2 %fusion.105 = f32[2048,1024]{1,0:T(8,128)} fusion(f32[512,1024]{1,0:T(8,128)S(1)} %copy-done.50, f32[512,2048]{1,0:T(8,128)S(1)} %copy-done.65, f32[512,2048]{1,0:T(8,128)S(1)} %copy-done.64, f32[2048]{0:T(1024)S(1)} %copy-done.117), kind=kOutput, calls=%fused_computation.156 | convolution fusion | flops 12888047616 | bytes 18882560 | tf_op jit(solution)/shard_map/transpose(jvp())/dot_general | solution.py:136
  649.9 6.9 convolution_bitcast_fusion
  656.8 7.1 convolution_bitcast_fusion.1
  663.8 6.9 convolution_bitcast_fusion.2
  680.9 11.0 fusion.3
  700.9 11.1 fusion
  712.1 10.6 multiply_reduce_fusion.1
  728.6 65.8 %all-reduce.12 = (f32[1024]{0:T(1024)}, f32[1024]{0:T(1024)}, f32[1024]{0:T(1024)}, f32[1024]{0:T(1024)}, f32[2048]{0:T(1024)}, /*index=5*/f32[1024]{0:T(1024)}) all-reduce(f32[1024]{0:T(1024)S(1)} %get-tuple-element.36, f32[1024]{0:T(1024)S(1)} %get-tuple-element.43, ...), channel_id=1, replica_groups=mesh['seq'=16,'mp'=2] {'seq'}, use_global_device_ids=true, to_apply=%region_17.18 | all-reduce | flops 7168 | bytes 57344 | tf_op jit(solution)/shard_map/psum | solution.py:240
  801.7 366.3 %all-reduce.27.cloned.1.call-done = (f32[3,1024,512]{2,1,0:T(8,128)}, f32[512,1024]{1,0:T(8,128)}, f32[1024,2048]{1,0:T(8,128)}, f32[2048,1024]{1,0:T(8,128)}) async-done(((f32[3,1024,512]{2,1,0:T(8,128)}, f32[512,1024]{1,0:T(8,128)}, f32[1024,2048]{1,0:T(8,128)}, f32[2048,1024]{1,0:T(8,128)}), (f32[3,1024,512]{2,1,0:T(8,128)}, f32[512,1024]{1,0:T(8,128)}, f32[1024,2048]{1,0:T(8,128)}, ...) | async-done | bytes 25165840 | tf_op jit(solution)/shard_map/psum | solution.py:240
  1168.0 6.9 copy.162
  (441 shorter events, 255.5 us)
Async XLA Ops:
  7.2 192.2 %copy-start = (bf16[512,1024]{1,0:T(8,128)(2,1)S(1)}, bf16[512,1024]{1,0:T(8,128)(2,1)}, u32[]{:S(2)}) copy-start(bf16[512,1024]{1,0:T(8,128)(2,1)} %param.26) | copy-start | bytes 3145732
  11.4 166.0 %copy-start.2 = (f32[512,1024]{1,0:T(8,128)}, f32[512,1024]{1,0:T(8,128)S(1)}, u32[]{:S(2)}) copy-start(f32[512,1024]{1,0:T(8,128)S(1)} %multiply_add_fusion.6) | copy-start | bytes 6291460
  15.8 30.4 %all-to-all-start = ((f32[16,32,512]{2,1,0:T(8,128)}), f32[16,32,512]{2,1,0:T(8,128)}, u32[]{:S(2)}, u32[]{:S(2)}) async-start(f32[16,32,512]{2,1,0:T(8,128)} %dynamic-slice_bitcast_fusion.1), calls=%async_computation | async-start | bytes 2097152 | tf_op jit(solution)/shard_map/all_to_all | solution.py:177
  23.2 147.9 %all-gather.3.cloned.1.call-start = ((), (), s32[]{:S(2)}) async-start(), calls=%async_computation.6 | async-start | bytes 3145728 | tf_op jit(solution)/shard_map/all_gather | solution.py:185
  23.3 69.9 %copy-start.109 = (f32[4096]{0:T(1024)}, f32[4096]{0:T(1024)S(1)}, u32[]{:S(2)}) copy-start(f32[4096]{0:T(1024)S(1)} %iota_convert_fusion) | copy-start | bytes 49156
  23.4 69.8 %copy-start.90 = (f32[2,32,16]{2,0,1:T(2,128)}, f32[2,32,16]{2,0,1:T(2,128)S(1)}, u32[]{:S(2)}) copy-start(f32[2,32,16]{2,0,1:T(2,128)S(1)} %copy.93) | copy-start | bytes 12292
  23.5 69.7 %copy-start.105 = (f32[32,16]{1,0:T(8,128)}, f32[32,16]{1,0:T(8,128)S(1)}, u32[]{:S(2)}) copy-start(f32[32,16]{1,0:T(8,128)S(1)} %get-tuple-element.72) | copy-start | bytes 6148
  23.5 69.7 %copy-start.107 = (f32[32,16]{1,0:T(8,128)}, f32[32,16]{1,0:T(8,128)S(1)}, u32[]{:S(2)}) copy-start(f32[32,16]{1,0:T(8,128)S(1)} %get-tuple-element.73) | copy-start | bytes 6148
  137.6 133.1 %all-reduce.21.cloned.1.call-start = ((), (), s32[]{:S(2)}) async-start(), calls=%async_computation.4 | async-start | bytes 4194304 | tf_op jit(solution)/shard_map/psum | solution.py:199
  175.2 4.1 collective-permute-start
  202.5 68.1 %copy-start.11 = (f32[512,1024]{1,0:T(8,128)S(1)}, f32[512,1024]{1,0:T(8,128)}, u32[]{:S(2)}) copy-start(f32[512,1024]{1,0:T(8,128)} %param.17) | copy-start | bytes 6291460
  202.6 172.0 %all-reduce.23.cloned.1.call-start = ((), (), s32[]{:S(2)}) async-start(), calls=%async_computation.5 | async-start | bytes 4194304 | tf_op jit(solution)/shard_map/psum | solution.py:206
  281.9 19.5 %copy-start.63 = (f32[512,2048]{1,0:T(8,128)}, f32[512,2048]{1,0:T(8,128)S(1)}, u32[]{:S(2)}) copy-start(f32[512,2048]{1,0:T(8,128)S(1)} %fusion.78) | copy-start | bytes 12582916
  311.4 63.1 %copy-start.18 = (f32[512,1024]{1,0:T(8,128)S(1)}, f32[512,1024]{1,0:T(8,128)}, u32[]{:S(2)}) copy-start(f32[512,1024]{1,0:T(8,128)} %copy-done.17) | copy-start | bytes 6291460
  311.5 173.4 %all-reduce.25.cloned.1.call-start = ((), (), s32[]{:S(2)}) async-start(), calls=%async_computation.7 | async-start | bytes 4194304
  409.8 3.8 collective-permute-start.1
  562.6 35.0 %all-to-all-start.3 = ((f32[32,16,512]{2,0,1:T(8,128)}), f32[32,16,512]{2,0,1:T(8,128)S(1)}, u32[]{:S(2)}, u32[]{:S(2)}) async-start(f32[32,16,512]{2,0,1:T(8,128)} %copy.107), calls=%async_computation.3 | async-start | bytes 2097152 | tf_op jit(solution)/shard_map/all_to_all | solution.py:232
  567.6 158.5 %all-reduce.29.cloned.1.call-start = ((), (), s32[]{:S(2)}) async-start(), calls=%async_computation.9 | async-start | bytes 8388608 | tf_op jit(solution)/shard_map/psum | solution.py:202
  567.8 12.2 %copy-start.74 = (f32[1,640,4,128]{1,3,2,0:T(8,128)S(1)}, f32[1,640,4,128]{1,3,2,0:T(8,128)}, u32[]{:S(2)}) copy-start(f32[1,640,4,128]{1,3,2,0:T(8,128)} %copy-done.73) | copy-start | bytes 3932164
  567.8 12.3 %copy-start.56 = (f32[1,640,4,128]{1,3,2,0:T(8,128)S(1)}, f32[1,640,4,128]{1,3,2,0:T(8,128)}, u32[]{:S(2)}) copy-start(f32[1,640,4,128]{1,3,2,0:T(8,128)} %copy-done.55) | copy-start | bytes 3932164
  580.1 11.8 slice-start.4
  610.5 557.5 %all-reduce.27.cloned.1.call-start = ((), (), s32[]{:S(2)}) async-start(), calls=%async_computation.8 | async-start | bytes 50331648 | tf_op jit(solution)/shard_map/psum | solution.py:240
  612.0 17.8 %copy-start.50 = (f32[512,1024]{1,0:T(8,128)S(1)}, f32[512,1024]{1,0:T(8,128)}, u32[]{:S(2)}) copy-start(f32[512,1024]{1,0:T(8,128)} %param.33) | copy-start | bytes 6291460
  612.0 17.8 %copy-start.64 = (f32[512,2048]{1,0:T(8,128)S(1)}, f32[512,2048]{1,0:T(8,128)}, u32[]{:S(2)}) copy-start(f32[512,2048]{1,0:T(8,128)} %copy-done.63) | copy-start | bytes 12582916
  612.0 17.8 %copy-start.65 = (f32[512,2048]{1,0:T(8,128)S(1)}, f32[512,2048]{1,0:T(8,128)}, u32[]{:S(2)}) copy-start(f32[512,2048]{1,0:T(8,128)} %get-tuple-element.58) | copy-start | bytes 12582916
  629.9 16.2 %copy-start.53 = (f32[1024,1,512]{0,2,1:T(8,128)S(1)}, f32[1024,1,512]{0,2,1:T(8,128)}, u32[]{:S(2)}) copy-start(f32[1024,1,512]{0,2,1:T(8,128)} %copy-done.52) | copy-start | bytes 6291460
  680.9 11.1 copy-start.28
  680.9 11.1 copy-start.29
  700.9 11.2 copy-start.91
  712.1 11.4 copy-start.83
  712.1 11.4 copy-start.31
  726.2 68.2 %copy-start.101 = (f32[512]{0:T(512)S(1)}, f32[512]{0:T(512)}, u32[]{:S(2)}) copy-start(f32[512]{0:T(512)} %copy-done.100) | copy-start | bytes 6148
  (116 other events, 427.6 us)
Sparse Core Ops, SparseCore 0:
  137.7 33.4 all-gather.2
  202.7 67.9 all-reduce.20
  311.6 62.9 all-reduce.22
  415.7 69.0 all-reduce.24
  610.6 108.5 all-reduce.28
  724.5 443.4 all-reduce.26
where the time goes:
time: 1200 us; the launch traced here: 1190 us
  waiting for transfers between devices  590 us (49%)
  matrix products  308 us (26%)
  blocking collectives  128 us (11%)
  local copies, waits for them, and re-layouts  99.9 us (8%)
  other arithmetic  34.4 us (3%)
  starting transfers between devices  16.5 us (1%)
  between operations  16.5 us (1%)
    psum x1, waiting for transfers between devices, per_device(): lax.psum((grad_gain1, grad_bias1, grad_qkv, grad_out, grad_gain2, grad_bi...  366 us
    dot_general x50, matrix products, product(): return jnp.einsum(form, left, right, precision=lax.Precision.HIGHEST)  140 us
    unnamed x7, waiting for transfers between devices  68.1 us
    psum x1, waiting for transfers between devices, per_device(): mixed = tokens + lax.psum(attn_part, 'mp')  67.9 us
    psum x1, blocking collectives, per_device(): lax.psum((grad_gain1, grad_bias1, grad_qkv, grad_out, grad_gain2, grad_bi...  65.8 us
    psum x1, waiting for transfers between devices, per_device(): grad_normed2 = lax.psum(grad_normed2_part, 'mp')  62 us
    dot_general x3, matrix products, feed_local(): return jnp.dot(hidden, down_w, precision=highest)  47.9 us
    unnamed x287, local copies, waits for them, and re-layouts  37.9 us
  transfers between devices with their start and end apart: 10, of which 7 were waited for; matrix products, arithmetic and copies ran while one was open for 15% of the time, Pallas kernels for 0%

commit v1 on v0

--- a/solution.py
+++ b/solution.py
@@ -3,12 +3,26 @@
 import jax.numpy as jnp
 from jax import lax
 from jax.sharding import PartitionSpec as P
+from jax.lax import axis_index, axis_size, ppermute
 
 HDIM = 128
 BLOCK = 512
 CTX = 128
 LEN = 4096
 epsilon = 1e-05
+
+
+def balance_rounds(point, dim_no, x_in):
+    low = point.shape
+    return jnp.moveaxis(
+        point.reshape(*low[:dim_no], x_in, low[dim_no] // x_in, *low[dim_no + 1 :]), dim_no, 0
+    )
+
+
+def check_pairs_all(packet, dim_i):
+    kept_arr = list(packet.shape[1:])
+    kept_arr[dim_i] *= packet.shape[0]
+    return jnp.moveaxis(packet, 0, dim_i).reshape(kept_arr)
 
 
 def from_behind(block, axis, distance):
@@ -180,7 +194,23 @@
         return ssm_local(time_rows, coef_in, coef_out, rates, skips, window_state)
 
     time_out, ssm_pull = jax.vjp(ssm_piece, time_in, in_coef, out_coef, decay_rate, skip_gain)
-    returned = lax.all_to_all(time_out, "seq", split_axis=1, concat_axis=0, tiled=True)
+    block_next = axis_size("seq")
+    t1 = axis_index("seq")
+    mid_arr, y2 = (block_next, t1)
+    o_now = balance_rounds(time_out, 1, mid_arr)
+    plain = o_now
+    i0 = 1
+    while i0 < mid_arr:
+        earlier, back = ((y2 + i0) % mid_arr, (y2 - i0) % mid_arr)
+        state_now = lax.dynamic_index_in_dim(o_now, earlier, 0)
+        next_value = ppermute(
+            state_now,
+            axis_name="seq",
+            perm=[(src_i, (src_i + i0) % mid_arr) for src_i in range(mid_arr)],
+        )
+        plain = lax.dynamic_update_slice_in_dim(plain, next_value, back, axis=0)
+        i0 += 1
+    returned = check_pairs_all(plain, 0)
     width_back = returned.shape[1]
     halves = lax.all_gather(
         returned.reshape(count_seq, 1, channels, width_back), "mp", axis=1, tiled=True

time: 1200 us -> 1220 us (1.017)
  blocking collectives: 128 us -> 95.9 us
  starting transfers between devices: 16.5 us -> 41.7 us
  local copies, waits for them, and re-layouts: 99.9 us -> 125 us
    all_to_all x1 -> x0, blocking collectives: 31.6 us -> none  [per_device(): lax.all_to_all(time_out, 'seq', split_axis=1, concat_axis=0, tiled=True)]
    ppermute x0 -> x15, starting transfers between devices: none -> 25.3 us  [per_device(): ppermute(state_now, axis_name='seq', perm=[(src_i, (src_i + i0) % mid_arr...]
    unnamed x287 -> x322, local copies, waits for them, and re-layouts: 37.9 us -> 40.9 us
  transfers between devices with their start and end apart: 10 -> 25, of which waited for: 7 -> 7; matrix products, arithmetic and copies ran while one was open for 15% -> 16% of each run, Pallas kernels for 0% -> 0%
where the time goes in v1:
time: 1220 us; the launch traced here: 1210 us
  waiting for transfers between devices  588 us (48%)
  matrix products  308 us (25%)
  local copies, waits for them, and re-layouts  125 us (10%)
  blocking collectives  95.9 us (8%)
  starting transfers between devices  41.7 us (3%)
  other arithmetic  38.1 us (3%)
  between operations  16.7 us (1%)
    psum x1, waiting for transfers between devices, per_device(): lax.psum((grad_gain1, grad_bias1, grad_qkv, grad_out, grad_gain2, grad_bi...  367 us
    dot_general x50, matrix products, product(): return jnp.einsum(form, left, right, precision=lax.Precision.HIGHEST)  141 us
    unnamed x7, waiting for transfers between devices  68.1 us
    psum x1, waiting for transfers between devices, per_device(): mixed = tokens + lax.psum(attn_part, 'mp')  67.9 us
    psum x1, blocking collectives, per_device(): lax.psum((grad_gain1, grad_bias1, grad_qkv, grad_out, grad_gain2, grad_bi...  65.6 us
    psum x1, waiting for transfers between devices, per_device(): grad_normed2 = lax.psum(grad_normed2_part, 'mp')  62.2 us
    dot_general x3, matrix products, feed_local(): return jnp.dot(hidden, down_w, precision=highest)  47.2 us
    unnamed x322, local copies, waits for them, and re-layouts  40.9 us
  transfers between devices with their start and end apart: 25, of which 7 were waited for; matrix products, arithmetic and copies ran while one was open for 16% of the time, Pallas kernels for 0%

profile of v1, /device:TPU:0, one launch (start us, length us, event | category | flops | bytes accessed | tf_op | source)
XLA Modules:
  0.0 1213.3 jit_solution(5934348725218581919)
XLA Ops:
  15.8 7.4 all-to-all-start
  23.8 5.4 fusion.2
  93.5 7.8 fusion.8
  104.4 5.6 constant_dynamic-slice_fusion
  167.1 15.6 %all-gather.2.cloned.1.call-done = f32[16,2,32,512]{3,2,1,0:T(8,128)} async-done(((f32[16,1,32,512]{3,2,1,0:T(8,128)}), f32[16,2,32,512]{3,2,1,0:T(8,128)}) %all-gather.2.cloned.1.call-update) | async-done | bytes 2097168 | tf_op jit(solution)/shard_map/all_gather | solution.py:215
  195.5 5.5 fusion.7
  203.3 6.3 fusion.28
  214.2 67.9 %all-reduce.21.cloned.1.call-done = f32[512,1024]{1,0:T(8,128)} async-done(((f32[512,1024]{1,0:T(8,128)}), f32[512,1024]{1,0:T(8,128)}) %all-reduce.21.cloned.1.call-update) | async-done | bytes 2097168 | tf_op jit(solution)/shard_map/psum | solution.py:229
  286.0 7.2 fusion.78
  293.3 19.4 %fusion.441 = (f32[2048]{0:T(1024)}, f32[512,2048]{1,0:T(8,128)S(1)}, f32[512,2048]{1,0:T(8,128)}) fusion(f32[512,2048]{1,0:T(8,128)S(1)} %fusion.78, f32[2048]{0:T(1024)S(1)} %copy-done.128, f32[512,1024]{1,0:T(8,128)S(1)} %copy-done.52, bf16[2048,1024]{1,0:T(8,128)(2,1)S(1)} %copy-done.137), kind=kOutput, calls=%fused_computation.546 | convolution fusion | flops 12961445888 | bytes 18890752 | tf_op jit(solution)/shard_map/transpose(jvp())/dot_general | solution.py:150
  314.7 8.0 fusion.450
  323.6 62.2 %all-reduce.23.cloned.1.call-done = f32[512,1024]{1,0:T(8,128)} async-done(((f32[512,1024]{1,0:T(8,128)}), f32[512,1024]{1,0:T(8,128)}) %all-reduce.23.cloned.1.call-update) | async-done | bytes 2097168 | tf_op jit(solution)/shard_map/psum | solution.py:236
  403.6 8.8 multiply_reduce_fusion.2
  431.7 68.0 %all-reduce.25.cloned.1.call-done = f32[16,2,32,512]{3,2,1,0:T(8,128)} async-done(((f32[16,2,32,512]{3,2,1,0:T(8,128)}), f32[16,2,32,512]{3,2,1,0:T(8,128)}) %all-reduce.25.cloned.1.call-update) | async-done | bytes 2097168
  501.7 30.3 %all_to_all.45 = f32[16,32,512]{2,1,0:T(8,128)S(1)} all-to-all(f32[16,32,512]{2,1,0:T(8,128)S(1)} %dynamic-slice_bitcast_fusion), channel_id=1, replica_groups=mesh['seq'=16,'mp'=2] {'seq'}, dimensions={0} | all-to-all | bytes 2097152 | tf_op jit(solution)/shard_map/all_to_all | solution.py:254
  551.4 5.0 multiply_reduce_fusion.4
  580.5 5.0 all-to-all-start.2
  585.8 11.9 fusion.106
  605.2 4.9 fusion.116
  610.2 6.6 fusion.109
  622.8 8.1 bitcast_add_fusion
  632.6 17.8 %fusion.77 = f32[1024,2048]{1,0:T(8,128)} fusion(f32[512,2048]{1,0:T(8,128)} %copy-done.141, f32[512,1024]{1,0:T(8,128)S(1)} %copy-done.19, f32[1024]{0:T(1024)S(1)} %copy-done.139, f32[1024]{0:T(1024)S(1)} %copy-done.127, f32[512]{0:T(512)S(1)} %copy-done.111, f32[512]{0:T(512)S(1)} %copy-done.108), kind=kOutput, calls=%fused_computation.127 | convolution fusion | flops 12886999040 | bytes 14692352 | tf_op jit(solution)/shard_map/transpose(jvp())/dot_general | solution.py:149
  650.4 16.0 %fusion.105 = f32[2048,1024]{1,0:T(8,128)} fusion(f32[512,1024]{1,0:T(8,128)S(1)} %copy-done.54, f32[512,2048]{1,0:T(8,128)S(1)} %copy-done.68, f32[512,2048]{1,0:T(8,128)S(1)} %copy-done.67, f32[2048]{0:T(1024)S(1)} %copy-done.129), kind=kOutput, calls=%fused_computation.156 | convolution fusion | flops 12888047616 | bytes 18882560 | tf_op jit(solution)/shard_map/transpose(jvp())/dot_general | solution.py:150
  670.1 6.7 convolution_bitcast_fusion
  676.8 7.1 convolution_bitcast_fusion.1
  683.9 6.7 convolution_bitcast_fusion.2
  700.6 11.0 fusion.3
  720.7 11.3 fusion
  732.1 10.6 multiply_reduce_fusion.1
  748.6 65.6 %all-reduce.12 = (f32[1024]{0:T(1024)}, f32[1024]{0:T(1024)}, f32[1024]{0:T(1024)}, f32[1024]{0:T(1024)}, f32[2048]{0:T(1024)}, /*index=5*/f32[1024]{0:T(1024)}) all-reduce(f32[1024]{0:T(1024)S(1)} %get-tuple-element.36, f32[1024]{0:T(1024)S(1)} %get-tuple-element.43, ...), channel_id=1, replica_groups=mesh['seq'=16,'mp'=2] {'seq'}, use_global_device_ids=true, to_apply=%region_17.18 | all-reduce | flops 7168 | bytes 57344 | tf_op jit(solution)/shard_map/psum | solution.py:270
  821.5 366.9 %all-reduce.27.cloned.1.call-done = (f32[3,1024,512]{2,1,0:T(8,128)}, f32[512,1024]{1,0:T(8,128)}, f32[1024,2048]{1,0:T(8,128)}, f32[2048,1024]{1,0:T(8,128)}) async-done(((f32[3,1024,512]{2,1,0:T(8,128)}, f32[512,1024]{1,0:T(8,128)}, f32[1024,2048]{1,0:T(8,128)}, f32[2048,1024]{1,0:T(8,128)}), (f32[3,1024,512]{2,1,0:T(8,128)}, f32[512,1024]{1,0:T(8,128)}, f32[1024,2048]{1,0:T(8,128)}, ...) | async-done | bytes 25165840 | tf_op jit(solution)/shard_map/psum | solution.py:270
  1188.5 6.9 copy.224
  (520 shorter events, 303.1 us)
Async XLA Ops:
  7.2 203.4 %copy-start = (bf16[512,1024]{1,0:T(8,128)(2,1)S(1)}, bf16[512,1024]{1,0:T(8,128)(2,1)}, u32[]{:S(2)}) copy-start(bf16[512,1024]{1,0:T(8,128)(2,1)} %param.26) | copy-start | bytes 3145732
  11.4 177.4 %copy-start.2 = (f32[512,1024]{1,0:T(8,128)}, f32[512,1024]{1,0:T(8,128)S(1)}, u32[]{:S(2)}) copy-start(f32[512,1024]{1,0:T(8,128)S(1)} %multiply_add_fusion.6) | copy-start | bytes 6291460
  15.8 30.4 %all-to-all-start = ((f32[16,32,512]{2,1,0:T(8,128)}), f32[16,32,512]{2,1,0:T(8,128)}, u32[]{:S(2)}, u32[]{:S(2)}) async-start(f32[16,32,512]{2,1,0:T(8,128)} %dynamic-slice_bitcast_fusion.1), calls=%async_computation | async-start | bytes 2097152 | tf_op jit(solution)/shard_map/all_to_all | solution.py:191
  23.2 159.5 %all-gather.2.cloned.1.call-start = ((), (), s32[]{:S(2)}) async-start(), calls=%async_computation.3 | async-start | bytes 3145728 | tf_op jit(solution)/shard_map/all_gather | solution.py:215
  23.3 70.1 %copy-start.121 = (f32[4096]{0:T(1024)}, f32[4096]{0:T(1024)S(1)}, u32[]{:S(2)}) copy-start(f32[4096]{0:T(1024)S(1)} %iota_convert_fusion) | copy-start | bytes 49156
  23.6 69.8 %copy-start.102 = (f32[2,32,16]{2,0,1:T(2,128)}, f32[2,32,16]{2,0,1:T(2,128)S(1)}, u32[]{:S(2)}) copy-start(f32[2,32,16]{2,0,1:T(2,128)S(1)} %copy.93) | copy-start | bytes 12292
  23.7 69.7 %copy-start.117 = (f32[32,16]{1,0:T(8,128)}, f32[32,16]{1,0:T(8,128)S(1)}, u32[]{:S(2)}) copy-start(f32[32,16]{1,0:T(8,128)S(1)} %get-tuple-element.87) | copy-start | bytes 6148
  23.7 69.7 %copy-start.119 = (f32[32,16]{1,0:T(8,128)}, f32[32,16]{1,0:T(8,128)S(1)}, u32[]{:S(2)}) copy-start(f32[32,16]{1,0:T(8,128)S(1)} %get-tuple-element.88) | copy-start | bytes 6148
  110.6 10.3 collective-permute-start
  114.2 10.6 collective-permute-start.1
  116.2 12.1 %collective-permute-start.2 = (f32[1,32,512]{2,1,0:T(8,128)S(1)}, f32[1,32,512]{2,1,0:T(8,128)S(1)}, u32[]{:S(2)}, u32[]{:S(2)}) collective-permute-start(f32[1,32,512]{2,1,0:T(8,128)S(1)} %bitcast.537), channel_id=1, source_target_pairs={{0,6},{2,8},{4,10},{6,12},{8,14},{10,16},{12,18},{14,20},{16,22},{... | collective-permute-start | bytes 196616 | tf_op jit(solution)/shard_map/ppermute | solution.py:206
  119.8 10.2 collective-permute-start.3
  120.6 11.0 collective-permute-start.4
  120.9 12.6 %collective-permute-start.5 = (f32[1,32,512]{2,1,0:T(8,128)S(1)}, f32[1,32,512]{2,1,0:T(8,128)S(1)}, u32[]{:S(2)}, u32[]{:S(2)}) collective-permute-start(f32[1,32,512]{2,1,0:T(8,128)S(1)} %bitcast.534), channel_id=1, source_target_pairs={{0,12},{2,14},{4,16},{6,18},{8,20},{10,22},{12,24},{14,26},{16,28}... | collective-permute-start | bytes 196616 | tf_op jit(solution)/shard_map/ppermute | solution.py:206
  124.8 12.5 %collective-permute-start.6 = (f32[1,32,512]{2,1,0:T(8,128)S(1)}, f32[1,32,512]{2,1,0:T(8,128)S(1)}, u32[]{:S(2)}, u32[]{:S(2)}) collective-permute-start(f32[1,32,512]{2,1,0:T(8,128)S(1)} %bitcast.533), channel_id=1, source_target_pairs={{0,14},{2,16},{4,18},{6,20},{8,22},{10,24},{12,26},{14,28},{16,30}... | collective-permute-start | bytes 196616 | tf_op jit(solution)/shard_map/ppermute | solution.py:206
  128.3 11.1 collective-permute-start.7
  130.0 10.4 collective-permute-start.8
  131.6 10.6 collective-permute-start.9
  133.5 12.7 %collective-permute-start.10 = (f32[1,32,512]{2,1,0:T(8,128)S(1)}, f32[1,32,512]{2,1,0:T(8,128)S(1)}, u32[]{:S(2)}, u32[]{:S(2)}) collective-permute-start(f32[1,32,512]{2,1,0:T(8,128)S(1)} %bitcast.529), channel_id=1, source_target_pairs={{0,22},{2,24},{4,26},{6,28},{8,30},{10,0},{12,2},{14,4},{16,6},{18... | collective-permute-start | bytes 196616 | tf_op jit(solution)/shard_map/ppermute | solution.py:206
  137.3 9.6 collective-permute-start.11
  139.5 8.1 collective-permute-start.12
  140.4 7.8 collective-permute-start.13
  142.2 6.6 collective-permute-start.14
  149.5 132.6 %all-reduce.21.cloned.1.call-start = ((), (), s32[]{:S(2)}) async-start(), calls=%async_computation.4 | async-start | bytes 4194304 | tf_op jit(solution)/shard_map/psum | solution.py:229
  186.8 3.9 collective-permute-start.15
  213.7 68.4 %copy-start.11 = (f32[512,1024]{1,0:T(8,128)S(1)}, f32[512,1024]{1,0:T(8,128)}, u32[]{:S(2)}) copy-start(f32[512,1024]{1,0:T(8,128)} %param.17) | copy-start | bytes 6291460
  213.7 172.1 %all-reduce.23.cloned.1.call-start = ((), (), s32[]{:S(2)}) async-start(), calls=%async_computation.5 | async-start | bytes 4194304 | tf_op jit(solution)/shard_map/psum | solution.py:236
  322.7 177.0 %all-reduce.25.cloned.1.call-start = ((), (), s32[]{:S(2)}) async-start(), calls=%async_computation.6 | async-start | bytes 4194304
  422.2 3.8 collective-permute-start.16
  580.5 36.2 %all-to-all-start.2 = ((f32[32,16,512]{2,0,1:T(8,128)}), f32[32,16,512]{2,0,1:T(8,128)}, u32[]{:S(2)}, u32[]{:S(2)}) async-start(f32[32,16,512]{2,0,1:T(8,128)} %copy.107), calls=%async_computation.2 | async-start | bytes 2097152 | tf_op jit(solution)/shard_map/all_to_all | solution.py:262
  585.5 160.6 %all-reduce.29.cloned.1.call-start = ((), (), s32[]{:S(2)}) async-start(), calls=%async_computation.8 | async-start | bytes 8388608 | tf_op jit(solution)/shard_map/psum | solution.py:232
  631.0 557.5 %all-reduce.27.cloned.1.call-start = ((), (), s32[]{:S(2)}) async-start(), calls=%async_computation.7 | async-start | bytes 50331648 | tf_op jit(solution)/shard_map/psum | solution.py:270
  (141 other events, 810.6 us)
Sparse Core Ops, SparseCore 0:
  149.6 33.0 all-gather.1
  213.9 68.1 all-reduce.20
  322.8 62.9 all-reduce.22
  430.6 69.0 all-reduce.24
  631.1 108.5 all-reduce.28
  745.0 443.4 all-reduce.26
